TPU v7x, 32 devices: a whole 2x2x4 slice. The times are simulated.
32 devices in a mesh: energy: 8 (over z, y), space: 4 (over x, core).
Axes of the slice: x: 2, y: 2, z: 4, core: 2. Of those that a mesh axis runs over, the one named last changes fastest.
Arguments:
- lesser: bfloat16 [2, 512, 4, 65536], P(None, 'energy', 'space'), may hold values from -6 to 6
- greater: bfloat16 [2, 512, 4, 65536], P(None, 'energy', 'space'), may hold values from -6 to 6
- vdiag: bfloat16 [4, 256, 256], P('space'), may hold values from -0.375 to 0.375
- vlower: bfloat16 [4, 256, 256], P('space'), may hold values from -0.375 to 0.375
- occupancy: int32 [4, 8], P('space'), may hold values from 1 to 32, 128 in all within a row
- tile_order: int32 [4, 512], P('space'), may hold values from 0 to 511, each once within a row
Outputs:
- interaction_diag: bfloat16 [2, 512, 4, 256, 256], P(None, 'energy', 'space')
- interaction_lower: bfloat16 [2, 512, 4, 256, 256], P(None, 'energy', 'space')
Inputs may be any that keep to these rules, and one draw needn't show every extreme that they name: `occupancy`: for each block, the entries sum to 128 and the largest is exactly 32. `tile_order`: each row is a permutation of the tile numbers.
All inputs are finite; a program needn't handle non-finite values.
Results may differ from a plain program's by a relative error of at most 0.015.
Values may be sent and summed in bfloat16 or wider, within the bound.
A program may use at most 448 MiB of HBM per device.

v0:
```python
import jax
import jax.numpy as jnp
from jax import lax
from jax.sharding import PartitionSpec as P

TILE = 128
NNZ = 128


def passed_along(value, axis, steps):
    count = lax.axis_size(axis)
    leading, last = (max(0, -steps), min(count, count - steps))
    return lax.ppermute(value, axis, [(source, source + steps) for source in range(leading, last)])


def split_table(table):
    upper = table.astype(jnp.bfloat16)
    rest = (table - upper.astype(jnp.float32)).astype(jnp.bfloat16)
    return (upper, rest)


def table_times(parts, data):
    first = jnp.dot(parts[0], data, preferred_element_type=jnp.float32)
    return first + jnp.dot(parts[1], data, preferred_element_type=jnp.float32)


def split_times(parts, data):
    upper, rest = split_table(data)
    total = jnp.dot(parts[0], upper, preferred_element_type=jnp.float32)
    total = total + jnp.dot(parts[0], rest, preferred_element_type=jnp.float32)
    return total + jnp.dot(parts[1], upper, preferred_element_type=jnp.float32)


def unpack_tiles(tiles, index, local_energies, n_tiles, width):
    field = jnp.zeros((2, local_energies, n_tiles + 1, tiles.shape[-1]), jnp.bfloat16)
    field = field.at[:, :, index, :].set(tiles)
    return field[:, :, :n_tiles, :].reshape(2, local_energies, width, width)


def per_device(lesser, greater, vdiag, vlower, occupancy, tile_order):
    group_size = lax.axis_size("energy")
    local_energies = lesser.shape[1]
    width = vdiag.shape[1]
    n_tiles = lesser.shape[3] // TILE
    most_tiles = 2 * NNZ // group_size
    counts = occupancy[0]
    tile_perm = tile_order[0]
    slot_ids = jnp.arange(most_tiles, dtype=jnp.int32)
    flat_slot = jnp.arange(group_size, dtype=jnp.int32)[:, None] * most_tiles + slot_ids[None, :]
    listing = jnp.where(slot_ids[None, :] < counts[:, None], tile_perm[flat_slot], n_tiles)
    slot_index = listing.reshape(-1)

    def pack(source):
        tiled = source.reshape(2, local_energies, n_tiles, TILE)
        padded = jnp.concatenate(
            [tiled, jnp.zeros((2, local_energies, 1, TILE), source.dtype)], axis=2
        )
        taken = jnp.take(padded, slot_index, axis=2)
        return taken.reshape(2, local_energies, group_size, most_tiles, TILE)

    lesser_got, greater_got = (
        lax.all_to_all(pack(lesser), "energy", split_axis=2, concat_axis=1, tiled=True),
        lax.all_to_all(pack(greater), "energy", split_axis=2, concat_axis=1, tiled=True),
    )
    energies = local_energies * group_size
    columns = most_tiles * TILE
    lesser_cols = lesser_got.reshape(2, energies, columns)
    greater_cols = greater_got.reshape(2, energies, columns)
    grid = jnp.arange(energies, dtype=jnp.int32)
    phase = (grid[:, None] * grid[None, :] % energies).astype(jnp.float32) * (
        2.0 * jnp.pi / energies
    )
    cos_parts = split_table(jnp.cos(phase))
    sin_parts = split_table(jnp.sin(phase))
    first_real = table_times(cos_parts, lesser_cols[0]) + table_times(sin_parts, lesser_cols[1])
    first_imag = table_times(cos_parts, lesser_cols[1]) - table_times(sin_parts, lesser_cols[0])
    second_real = table_times(cos_parts, greater_cols[0]) - table_times(sin_parts, greater_cols[1])
    second_imag = table_times(cos_parts, greater_cols[1]) + table_times(sin_parts, greater_cols[0])
    product_real = first_real * second_real - first_imag * second_imag
    product_imag = first_real * second_imag + first_imag * second_real
    stacked = jnp.concatenate([product_real, product_imag], axis=1)
    cos_side = split_times(cos_parts, stacked)
    sin_side = split_times(sin_parts, stacked)
    factor = float(energies) ** (-1.5)
    polar_real = factor * (cos_side[:, :columns] - sin_side[:, columns:])
    polar_imag = factor * (cos_side[:, columns:] + sin_side[:, :columns])
    polar_tiles = jnp.stack([polar_real, polar_imag]).astype(jnp.bfloat16)
    polar_tiles = polar_tiles.reshape(2, group_size, local_energies, 1, most_tiles, TILE)
    returned = lax.all_to_all(polar_tiles, "energy", split_axis=1, concat_axis=3, tiled=True)
    returned = returned.reshape(2, local_energies, group_size * most_tiles, TILE)
    own_block = unpack_tiles(returned, slot_index, local_energies, n_tiles, width)
    diag_here = vdiag[0]
    lower_here = vlower[0]
    below_polar, below_diag = passed_along((own_block, diag_here), "space", 1)
    above_polar, above_lower = passed_along((own_block, lower_here), "space", -1)
    left_prod = jnp.einsum(
        "ab,xebc->xeac", lower_here, below_polar, preferred_element_type=jnp.float32
    ).astype(jnp.bfloat16)
    middle_prod = jnp.einsum(
        "ab,xebc->xeac", diag_here, own_block, preferred_element_type=jnp.float32
    ).astype(jnp.bfloat16)
    right_prod = jnp.einsum(
        "ba,xebc->xeac", above_lower, above_polar, preferred_element_type=jnp.float32
    ).astype(jnp.bfloat16)
    diag_sum = jnp.einsum(
        "xeab,cb->xeac", left_prod, lower_here, preferred_element_type=jnp.float32
    )
    diag_sum = diag_sum + jnp.einsum(
        "xeab,bc->xeac", middle_prod, diag_here, preferred_element_type=jnp.float32
    )
    diag_sum = diag_sum + jnp.einsum(
        "xeab,bc->xeac", right_prod, above_lower, preferred_element_type=jnp.float32
    )
    lower_sum = jnp.einsum(
        "xeab,bc->xeac", left_prod, below_diag, preferred_element_type=jnp.float32
    )
    lower_sum = lower_sum + jnp.einsum(
        "xeab,cb->xeac", middle_prod, lower_here, preferred_element_type=jnp.float32
    )
    diag_out = diag_sum.astype(jnp.bfloat16).reshape(2, local_energies, 1, width, width)
    lower_out = lower_sum.astype(jnp.bfloat16).reshape(2, local_energies, 1, width, width)
    return (diag_out, lower_out)


def solution(mesh):
    return jax.shard_map(
        per_device,
        mesh=mesh,
        in_specs=(
            P(None, "energy", "space", None),
            P(None, "energy", "space", None),
            P("space", None, None),
            P("space", None, None),
            P("space", None),
            P("space", None),
        ),
        out_specs=(P(None, "energy", "space", None, None), P(None, "energy", "space", None, None)),
        check_vma=False,
    )
```

profile of v0, /device:TPU:1, one launch (start us, length us, event | category | flops | bytes accessed | tf_op | source)
XLA Modules:
  0.0 1498.7 jit_solution(4860167797015654437)
XLA Ops:
  13.9 37.2 %copy.60 = bf16[2,64,512,128]{3,1,2,0:T(8,128)(2,1)S(1)} copy(bf16[2,64,512,128]{3,2,1,0:T(8,128)(2,1)S(1)} %bitcast.170) | data formatting | bytes 33554432 | tf_op jit(solution)/shard_map/reshape | solution.py:54
  60.8 40.3 %copy.62 = bf16[2,64,512,128]{3,1,2,0:T(8,128)(2,1)} copy(bf16[2,64,512,128]{3,2,1,0:T(8,128)(2,1)S(1)} %bitcast.171) | data formatting | bytes 33554432 | tf_op jit(solution)/shard_map/reshape | solution.py:54
  196.2 168.3 %all-to-all-done.1 = bf16[2,64,8,32,128]{4,3,1,0,2:T(8,128)(2,1)} async-done(((bf16[2,64,8,32,128]{4,3,1,0,2:T(8,128)(2,1)}), bf16[2,64,8,32,128]{4,3,1,0,2:T(8,128)(2,1)}, u32[]{:S(2)}, u32[]{:S(2)}) %all-to-all-start.1) | async-done | bytes 8388640 | tf_op jit(solution)/shard_map/all_to_all | solution.py:63
  393.3 157.9 %all-to-all-done = bf16[2,64,8,32,128]{4,3,1,0,2:T(8,128)(2,1)} async-done(((bf16[2,64,8,32,128]{4,3,1,0,2:T(8,128)(2,1)}), bf16[2,64,8,32,128]{4,3,1,0,2:T(8,128)(2,1)}, u32[]{:S(2)}, u32[]{:S(2)}) %all-to-all-start) | async-done | bytes 8388640 | tf_op jit(solution)/shard_map/all_to_all | solution.py:62
  661.5 18.6 %add_add_fusion.3 = f32[512,4096]{1,0:T(8,128)} fusion(f32[512,4096]{1,0:T(8,128)} %fusion.43, f32[512,4096]{1,0:T(8,128)} %fusion.50, f32[512,4096]{1,0:T(8,128)} %fusion.48, bf16[64,8,32,128]{3,2,1,0:T(8,128)(2,1)} %bitcast.192), kind=kOutput, calls=%fused_computation.37 | convolution fusion | flops 2158493696 | bytes 37748736 | tf_op jit(solution)/shard_map/dot_general | solution.py:24
  680.1 15.8 %add_add_fusion.2 = f32[512,4096]{1,0:T(8,128)} fusion(f32[512,4096]{1,0:T(8,128)} %fusion.32, f32[512,4096]{1,0:T(8,128)} %fusion.26, f32[512,4096]{1,0:T(8,128)} %fusion.24, bf16[64,8,32,128]{3,2,1,0:T(8,128)(2,1)S(1)} %bitcast.180), kind=kOutput, calls=%fused_computation.34 | convolution fusion | flops 2158493696 | bytes 37748736 | tf_op jit(solution)/shard_map/dot_general | solution.py:24
  695.9 25.6 %multiply_subtract_fusion = (f32[512,4096]{1,0:T(8,128)}, f32[512,4096]{1,0:T(8,128)}) fusion(f32[512,4096]{1,0:T(8,128)} %add_add_fusion.2, f32[512,4096]{1,0:T(8,128)} %add_add_fusion.3, f32[512,4096]{1,0:T(8,128)S(1)} %add_subtract_fusion.1, f32[512,4096]{1,0:T(8,128)} %fusion.46, bf16[64,8,32,128]{3,2,1,0:T(8,128)(2,1)} %bitcast.184, ...), kind=kOutput, calls=%fused_computation.33 | convolution fusion | flops 2171076608 | bytes 71303168 | tf_op jit(solution)/shard_map/dot_general | solution.py:24
  721.5 19.7 %fusion.77 = f32[512,8192]{1,0:T(8,128)} fusion(f32[512,4096]{1,0:T(8,128)} %get-tuple-element.16, f32[512,4096]{1,0:T(8,128)} %get-tuple-element.15), kind=kOutput, calls=%fused_computation.100 | convolution fusion | flops 4319870976 | bytes 33554432 | tf_op jit(solution)/shard_map/dot_general | solution.py:30
  741.2 19.8 %fusion.79 = f32[512,8192]{1,0:T(8,128)} fusion(f32[512,4096]{1,0:T(8,128)} %get-tuple-element.16, f32[512,4096]{1,0:T(8,128)} %get-tuple-element.15), kind=kOutput, calls=%fused_computation.101 | convolution fusion | flops 4315676672 | bytes 33554432 | tf_op jit(solution)/shard_map/dot_general | solution.py:29
  761.0 20.1 %fusion.86 = f32[512,8192]{1,0:T(8,128)} fusion(f32[512,4096]{1,0:T(8,128)} %get-tuple-element.16, f32[512,4096]{1,0:T(8,128)} %get-tuple-element.15), kind=kOutput, calls=%fused_computation.103 | convolution fusion | flops 4319870976 | bytes 33554432 | tf_op jit(solution)/shard_map/dot_general | solution.py:30
  781.1 20.5 %fusion.88 = f32[512,8192]{1,0:T(8,128)} fusion(f32[512,4096]{1,0:T(8,128)} %get-tuple-element.16, f32[512,4096]{1,0:T(8,128)} %get-tuple-element.15), kind=kOutput, calls=%fused_computation.104 | convolution fusion | flops 4315676672 | bytes 33554432 | tf_op jit(solution)/shard_map/dot_general | solution.py:29
  801.6 23.8 %add_add_fusion.1 = f32[512,8192]{1,0:T(8,128)} fusion(f32[512,8192]{1,0:T(8,128)} %fusion.79, f32[512,8192]{1,0:T(8,128)} %fusion.77, f32[512,4096]{1,0:T(8,128)} %get-tuple-element.16, f32[512,4096]{1,0:T(8,128)} %get-tuple-element.15), kind=kOutput, calls=%fused_computation.17 | convolution fusion | flops 4324851712 | bytes 67108864 | tf_op jit(solution)/shard_map/dot_general | solution.py:31
  825.4 23.7 %add_add_fusion = f32[512,8192]{1,0:T(8,128)} fusion(f32[512,8192]{1,0:T(8,128)} %fusion.88, f32[512,8192]{1,0:T(8,128)} %fusion.86, f32[512,4096]{1,0:T(8,128)} %get-tuple-element.16, f32[512,4096]{1,0:T(8,128)} %get-tuple-element.15), kind=kOutput, calls=%fused_computation.16 | convolution fusion | flops 4324851712 | bytes 67108864 | tf_op jit(solution)/shard_map/dot_general | solution.py:31
  880.6 181.0 %all-to-all-done.2 = bf16[2,8,64,1,32,128]{5,4,2,3,0,1:T(8,128)(2,1)} async-done(((bf16[2,8,64,1,32,128]{5,4,2,3,0,1:T(8,128)(2,1)}), bf16[2,8,64,1,32,128]{5,4,2,3,0,1:T(8,128)(2,1)}, u32[]{:S(2)}, u32[]{:S(2)}) %all-to-all-start.2) | async-done | bytes 8388640 | tf_op jit(solution)/shard_map/all_to_all | solution.py:89
  1089.3 40.8 %scatter_fusion = bf16[2,64,513,128]{3,1,2,0:T(8,128)(2,1)} fusion(bf16[2,64,513,128]{3,1,2,0:T(8,128)(2,1)} %broadcast_in_dim.13, s32[256]{0:T(256)S(1)} %bitcast.197, bf16[256,2,64,128]{3,2,1,0:T(8,128)(2,1)} %copy.67), kind=kCustom, calls=%fused_computation.3 | custom fusion | bytes 25166848 | tf_op jit(solution)/shard_map/scatter | solution.py:36
  1138.2 36.2 %copy.68 = bf16[2,64,512,128]{3,2,1,0:T(8,128)(2,1)} copy(bf16[2,64,512,128]{3,1,2,0:T(8,128)(2,1)S(1)} %slice.58) | data formatting | bytes 33554432 | tf_op jit(solution)/shard_map/slice | solution.py:37
  1174.4 24.4 %reshape.176 = bf16[2,64,256,256]{3,2,1,0:T(8,128)(2,1)} reshape(bf16[2,64,512,128]{3,2,1,0:T(8,128)(2,1)} %copy.68) | data formatting | bytes 33554432 | tf_op jit(solution)/shard_map/reshape | solution.py:37
  1198.8 21.2 %copy.69 = bf16[2,64,256,256]{2,3,1,0:T(8,128)(2,1)} copy(bf16[2,64,256,256]{3,2,1,0:T(8,128)(2,1)} %reshape.176) | data formatting | bytes 33554432 | tf_op jit(solution)/shard_map/reshape | solution.py:37
  1249.3 21.4 %fusion.1 = f32[2,64,256,256]{3,2,1,0:T(8,128)} fusion(bf16[2,64,256,256]{3,2,1,0:T(8,128)(2,1)} %convolution_convert_fusion, bf16[1,256,256]{2,1,0:T(8,128)(2,1)S(1)} %copy-done.9), kind=kOutput, calls=%fused_computation.8 | convolution fusion | flops 4294967296 | bytes 50462720 | tf_op jit(solution)/shard_map/xeab,cb->xeac/dot_general | solution.py:117
  1270.7 21.4 %fusion.3 = f32[2,64,256,256]{3,2,1,0:T(8,128)} fusion(bf16[2,64,256,256]{3,2,1,0:T(8,128)(2,1)} %convolution_convert_fusion, bf16[1,256,256]{2,1,0:T(8,128)(2,1)S(1)} %copy-done.10), kind=kOutput, calls=%fused_computation.10 | convolution fusion | flops 4294967296 | bytes 50462720 | tf_op jit(solution)/shard_map/xeab,bc->xeac/dot_general | solution.py:108
  1292.1 114.8 %collective-permute-done = bf16[2,64,256,256]{2,3,1,0:T(8,128)(2,1)} collective-permute-done((bf16[2,64,256,256]{2,3,1,0:T(8,128)(2,1)}, bf16[2,64,256,256]{2,3,1,0:T(8,128)(2,1)}, u32[]{:S(2)}, u32[]{:S(2)}) %collective-permute-start) | collective-permute-done | bytes 16777248 | tf_op jit(solution)/shard_map/ppermute | solution.py:13
  1419.0 21.4 %fusion.6 = f32[2,64,256,256]{3,2,1,0:T(8,128)} fusion(bf16[2,64,256,256]{3,2,1,0:T(8,128)(2,1)} %convolution_convert_fusion.1, bf16[1,256,256]{2,1,0:T(8,128)(2,1)S(1)} %copy-done.9), kind=kOutput, calls=%fused_computation.13 | convolution fusion | flops 4294967296 | bytes 50462720 | tf_op jit(solution)/shard_map/xeab,cb->xeac/dot_general | solution.py:105
  1440.4 23.6 %fusion.12 = bf16[2,64,1,256,256]{4,3,2,1,0:T(8,128)(2,1)} fusion(f32[2,64,256,256]{3,2,1,0:T(8,128)} %fusion.1, bf16[2,64,256,256]{3,2,1,0:T(8,128)(2,1)} %convolution_convert_fusion.1, bf16[256,256]{1,0:T(8,128)(2,1)S(1)} %collective-permute-done.3), kind=kOutput, calls=%fused_computation.23 | convolution fusion | flops 4311744512 | bytes 67239936 | tf_op jit(solution)/shard_map/xeab,bc->xeac/dot_general | solution.py:114
  1464.1 34.5 %fusion.15 = bf16[2,64,1,256,256]{4,3,2,1,0:T(8,128)(2,1)} fusion(bf16[2,64,256,256]{2,3,1,0:T(8,128)(2,1)} %collective-permute-done.1, f32[2,64,256,256]{3,2,1,0:T(8,128)} %fusion.6, f32[2,64,256,256]{3,2,1,0:T(8,128)} %fusion.3, bf16[256,256]{1,0:T(8,128)(2,1)S(1)} %collective-permute-done.2), kind=kOutput, calls=%fused_computation.24 | convolution fusion | flops 8623489024 | bytes 100794368 | tf_op jit(solution)/shard_map/xeab,bc->xeac/dot_general | solution.py:111
  (83 shorter events, 365.5 us)
Async XLA Ops:
  0.6 0.7 copy-start
  4.1 9.8 copy-start.11
  101.1 11.5 copy-start.2
  175.7 188.8 %all-to-all-start.1 = ((bf16[2,64,8,32,128]{4,3,1,0,2:T(8,128)(2,1)}), bf16[2,64,8,32,128]{4,3,1,0,2:T(8,128)(2,1)}, u32[]{:S(2)}, u32[]{:S(2)}) async-start(bf16[2,64,8,32,128]{4,3,1,0,2:T(8,128)(2,1)} %copy.63), calls=%async_computation.1 | async-start | bytes 16777216 | tf_op jit(solution)/shard_map/all_to_all | solution.py:63
  364.6 186.6 %all-to-all-start = ((bf16[2,64,8,32,128]{4,3,1,0,2:T(8,128)(2,1)}), bf16[2,64,8,32,128]{4,3,1,0,2:T(8,128)(2,1)}, u32[]{:S(2)}, u32[]{:S(2)}) async-start(bf16[2,64,8,32,128]{4,3,1,0,2:T(8,128)(2,1)} %copy.61), calls=%async_computation | async-start | bytes 16777216 | tf_op jit(solution)/shard_map/all_to_all | solution.py:62
  375.5 8.9 copy-start.3
  555.4 72.6 %copy-start.7 = (bf16[1,8,64,1,32,128]{5,4,2,0,1,3:T(8,128)(2,1)}, bf16[1,8,64,1,32,128]{5,4,2,0,1,3:T(8,128)(2,1)S(1)}, u32[]{:S(2)}) copy-start(bf16[1,8,64,1,32,128]{5,4,2,0,1,3:T(8,128)(2,1)S(1)} %get-tuple-element.19) | copy-start | bytes 12582916
  555.4 81.5 %copy-start.5 = (bf16[1,8,64,1,32,128]{5,4,2,0,1,3:T(8,128)(2,1)}, bf16[1,8,64,1,32,128]{5,4,2,0,1,3:T(8,128)(2,1)S(1)}, u32[]{:S(2)}) copy-start(bf16[1,8,64,1,32,128]{5,4,2,0,1,3:T(8,128)(2,1)S(1)} %get-tuple-element.20) | copy-start | bytes 12582916
  564.6 8.9 copy-start.6
  591.8 9.0 copy-start.4
  865.1 3.3 copy-start.8
  874.7 5.7 copy-start.12
  874.7 186.9 %all-to-all-start.2 = ((bf16[2,8,64,1,32,128]{5,4,2,3,0,1:T(8,128)(2,1)}), bf16[2,8,64,1,32,128]{5,4,2,3,0,1:T(8,128)(2,1)}, u32[]{:S(2)}, u32[]{:S(2)}) async-start(bf16[2,8,64,1,32,128]{5,4,2,3,0,1:T(8,128)(2,1)} %pad_maximum_fusion.1), calls=%async_computation.2 | async-start | bytes 16777216 | tf_op jit(solution)/shard_map/all_to_all | solution.py:89
  1198.8 33.7 %copy-start.10 = (bf16[1,256,256]{2,1,0:T(8,128)(2,1)S(1)}, bf16[1,256,256]{2,1,0:T(8,128)(2,1)}, u32[]{:S(2)}) copy-start(bf16[1,256,256]{2,1,0:T(8,128)(2,1)} %param.10) | copy-start | bytes 393220
  1198.8 35.7 %copy-start.9 = (bf16[1,256,256]{2,1,0:T(8,128)(2,1)S(1)}, bf16[1,256,256]{2,1,0:T(8,128)(2,1)}, u32[]{:S(2)}) copy-start(bf16[1,256,256]{2,1,0:T(8,128)(2,1)} %param.11) | copy-start | bytes 393220
  1220.0 186.9 %collective-permute-start = (bf16[2,64,256,256]{2,3,1,0:T(8,128)(2,1)}, bf16[2,64,256,256]{2,3,1,0:T(8,128)(2,1)}, u32[]{:S(2)}, u32[]{:S(2)}) collective-permute-start(bf16[2,64,256,256]{2,3,1,0:T(8,128)(2,1)} %copy.69), channel_id=1, source_target_pairs={{0,1},{1,2},{2,3},{4,5},{5,6},{6,7},{8,9},{9,10},{10,11},{12,13},{... | collective-permute-start | bytes 50331656 | tf_op jit(solution)/shard_map/ppermute | solution.py:13
  1226.4 237.7 %collective-permute-start.1 = (bf16[2,64,256,256]{2,3,1,0:T(8,128)(2,1)}, bf16[2,64,256,256]{2,3,1,0:T(8,128)(2,1)}, u32[]{:S(2)}, u32[]{:S(2)}) collective-permute-start(bf16[2,64,256,256]{2,3,1,0:T(8,128)(2,1)} %copy.69), channel_id=1, source_target_pairs={{1,0},{2,1},{3,2},{5,4},{6,5},{7,6},{9,8},{10,9},{11,10},{13,12},{... | collective-permute-start | bytes 50331656 | tf_op jit(solution)/shard_map/ppermute | solution.py:13
  1232.6 207.9 %collective-permute-start.3 = (bf16[256,256]{1,0:T(8,128)(2,1)S(1)}, bf16[256,256]{1,0:T(8,128)(2,1)S(1)}, u32[]{:S(2)}, u32[]{:S(2)}) collective-permute-start(bf16[256,256]{1,0:T(8,128)(2,1)S(1)} %bitcast.196), channel_id=1, source_target_pairs={{0,1},{1,2},{2,3},{4,5},{5,6},{6,7},{8,9},{9,10},{10,11},{12,13},{... | collective-permute-start | bytes 393224 | tf_op jit(solution)/shard_map/ppermute | solution.py:13
  1234.5 229.6 %collective-permute-start.2 = (bf16[256,256]{1,0:T(8,128)(2,1)S(1)}, bf16[256,256]{1,0:T(8,128)(2,1)S(1)}, u32[]{:S(2)}, u32[]{:S(2)}) collective-permute-start(bf16[256,256]{1,0:T(8,128)(2,1)S(1)} %bitcast.195), channel_id=1, source_target_pairs={{1,0},{2,1},{3,2},{5,4},{6,5},{7,6},{9,8},{10,9},{11,10},{13,12},{... | collective-permute-start | bytes 393224 | tf_op jit(solution)/shard_map/ppermute | solution.py:13
  1464.1 34.5 %copy-start.1 = (s32[1,512]{1,0:T(1,128)S(1)}, s32[1,512]{1,0:T(1,128)}, u32[]{:S(2)}) copy-start(s32[1,512]{1,0:T(1,128)} %param.13) | copy-start | bytes 6148
where the time goes:
time: 1510 us; the launch traced here: 1500 us
  waiting for transfers between devices  622 us (41%)
  matrix products  458 us (30%)
  local copies, waits for them, and re-layouts  351 us (23%)
  starting transfers between devices  34.6 us (2%)
  other arithmetic  31.8 us (2%)
    all_to_all x1, waiting for transfers between devices, per_device(): lax.all_to_all(polar_tiles, 'energy', split_axis=1, concat_axis=3, tiled=...  181 us
    all_to_all x1, waiting for transfers between devices, per_device(): lax.all_to_all(pack(greater), 'energy', split_axis=2, concat_axis=1, tile...  168 us
    all_to_all x1, waiting for transfers between devices, per_device(): lax.all_to_all(pack(lesser), 'energy', split_axis=2, concat_axis=1, tiled...  158 us
    ppermute x4, waiting for transfers between devices, passed_along(): lax.ppermute(value, axis, [(source, source + steps) for source in range(l...  115 us
    dot_general x8, matrix products, table_times(): return first + jnp.dot(parts[1], data, preferred_element_type=jnp.float32)  112 us
    reshape x2, local copies, waits for them, and re-layouts, pack(): tiled = source.reshape(2, local_energies, n_tiles, TILE)  77.6 us
    dot_general x8, matrix products, table_times(): first = jnp.dot(parts[0], data, preferred_element_type=jnp.float32)  72.2 us
    dot_general x2, matrix products, split_times(): return total + jnp.dot(parts[1], upper, preferred_element_type=jnp.float32)  47.5 us
  transfers between devices with their start and end apart: 7, of which 4 were waited for; matrix products, arithmetic and copies ran while one was open for 10% of the time, Pallas kernels for 0%

commit v1 on v0

v1 whole, which is shorter than its diff:
```python
import functools

import jax
import jax.numpy as jnp
import numpy as np
from jax import lax
from jax.experimental import pallas as pl
from jax.experimental.pallas import tpu as pltpu
from jax.sharding import PartitionSpec as P

TILE = 128
NNZ = 128
BF16 = jnp.bfloat16
F32 = jnp.float32


def passed_along(value, axis, steps):
    count = lax.axis_size(axis)
    leading, last = (max(0, -steps), min(count, count - steps))
    return lax.ppermute(value, axis, [(source, source + steps) for source in range(leading, last)])


def fourier_table(energies):
    grid = np.arange(energies)
    phase = 2.0 * np.pi * ((grid[:, None] * grid[None, :]) % energies) / energies
    cos, sin = np.cos(phase), np.sin(phase)
    return jnp.asarray(np.block([[cos, sin], [-sin, cos]]), BF16)


def pack_body(ranks, most, per_rank, first, slots, counts, order, lesser, greater, packed, listing, stage, sem, out_sem):
    def rank_step(r, j):
        def slot_step(s, j):
            tile = order[r * most + s]
            listing[j] = tile
            slot = j % per_rank - first

            @pl.when((slot >= 0) & (slot < slots))
            def _():
                columns = pl.ds(pl.multiple_of(tile * TILE, TILE), TILE)
                for which, source in enumerate((lesser, greater)):
                    pltpu.make_async_copy(
                        source.at[:, :, columns], stage.at[j // per_rank, slot, which], sem
                    ).start()

            return j + 1

        return lax.fori_loop(0, counts[r], slot_step, j)

    lax.fori_loop(0, ranks, rank_step, 0)
    pltpu.make_async_copy(stage, stage, sem).wait()
    written = pltpu.make_async_copy(stage, packed, out_sem)
    written.start()
    written.wait()


def pack(counts, order, lesser, greater, ranks, per_rank, first, slots):
    local = lesser.shape[1]
    anywhere = pl.BlockSpec(memory_space=pl.ANY)
    scalars = pl.BlockSpec(memory_space=pltpu.SMEM)
    moved = 2 * ranks * slots * 4 * local * TILE * 2
    return pl.pallas_call(
        functools.partial(pack_body, ranks, 2 * NNZ // ranks, per_rank, first, slots),
        out_shape=(
            jax.ShapeDtypeStruct((ranks, slots, 2, 2, local, TILE), BF16),
            jax.ShapeDtypeStruct((NNZ,), jnp.int32),
        ),
        in_specs=[scalars, scalars, anywhere, anywhere],
        out_specs=(anywhere, scalars),
        scratch_shapes=[
            pltpu.VMEM((ranks, slots, 2, 2, local, TILE), BF16),
            pltpu.SemaphoreType.DMA,
            pltpu.SemaphoreType.DMA,
        ],
        compiler_params=pltpu.CompilerParams(vmem_limit_bytes=16 << 20),
        cost_estimate=pl.CostEstimate(flops=0, bytes_accessed=moved, transcendentals=0),
        name="pack",
    )(counts, order, lesser, greater)


def correlate_body(tiles, halves, factor, table, data, *rest):
    outs = rest[-halves:]
    ranks, _, _, _, local, _ = data.shape
    energies = ranks * local

    def part(tile, which, p):
        value = data[:, tile, which, p]
        if local % 16:
            return value.astype(F32).reshape(energies, TILE).astype(BF16)
        return value.reshape(energies, TILE)

    def columns(which, order):
        return jnp.concatenate(
            [jnp.concatenate([part(t, which, p) for p in order], axis=0) for t in range(tiles)],
            axis=1,
        )

    first = jnp.dot(table[...], columns(0, (0, 1)), preferred_element_type=F32)
    second = jnp.dot(table[...], columns(1, (1, 0)), preferred_element_type=F32)
    first_re, first_im = first[:energies], first[energies:]
    second_im, second_re = second[:energies], second[energies:]
    product = jnp.concatenate(
        [
            (first_re * second_im + first_im * second_re).astype(BF16),
            (first_re * second_re - first_im * second_im).astype(BF16),
        ],
        axis=0,
    )
    polar = jnp.dot(table[...], product, preferred_element_type=F32) * factor
    step = local // halves
    for t in range(tiles):
        for p in range(2):
            value = polar[(1 - p) * energies:(2 - p) * energies, t * TILE:(t + 1) * TILE]
            value = value.reshape(ranks, local, TILE).astype(BF16)
            for h in range(halves):
                outs[h][:, t, p] = value[:, h * step:(h + 1) * step]


def correlate(table, data, per_rank, first, halves, previous):
    ranks, slots, _, _, local, _ = data.shape
    energies = ranks * local
    tiles = 2 if slots % 2 == 0 else 1
    step = local // halves
    block = (ranks, tiles, 2, step, TILE)
    base = first // tiles
    flops = 2 * 3 * (2 * energies) ** 2 * slots * TILE
    return pl.pallas_call(
        functools.partial(correlate_body, tiles, halves, float(energies) ** -1.5),
        grid=(slots // tiles,),
        out_shape=[jax.ShapeDtypeStruct((ranks, per_rank, 2, step, TILE), BF16)] * halves,
        in_specs=[
            pl.BlockSpec(table.shape, lambda g: (0, 0)),
            pl.BlockSpec((ranks, tiles, 2, 2, local, TILE), lambda g: (0, g, 0, 0, 0, 0)),
        ]
        + [pl.BlockSpec(memory_space=pl.ANY)] * len(previous),
        out_specs=[pl.BlockSpec(block, lambda g: (0, base + g, 0, 0, 0))] * halves,
        input_output_aliases={2 + h: h for h in range(len(previous))},
        compiler_params=pltpu.CompilerParams(vmem_limit_bytes=48 << 20),
        cost_estimate=pl.CostEstimate(flops=flops, bytes_accessed=12 << 20, transcendentals=0),
        name="correlate",
    )(table, data, *previous)


def sandwich_body(count, own, below, above, even, left_w, own_w, right_w, outer, *rest):
    diag_out, lower_out = rest[-2:]

    def spread(tiles, which):
        mask = even[which]
        zero = jnp.zeros((), BF16)
        halves = [jnp.where(mask > 0.5, tiles, zero), jnp.where(mask > 0.5, zero, tiles)]
        return jnp.concatenate(halves, axis=1)

    def times(tiles, which, matrix):
        stacked = jnp.concatenate([spread(tiles[0, k], which) for k in range(count)], axis=0)
        return jnp.dot(stacked, matrix[...], preferred_element_type=F32).astype(BF16)

    low, mid, top = times(below, 0, left_w), times(own, 1, own_w), times(above, 2, right_w)
    for k in range(count):
        here = slice(k * NNZ, (k + 1) * NNZ)
        inner = jnp.concatenate([low[here], mid[here]], axis=0)
        both = jnp.dot(outer[:, : 2 * NNZ], inner, preferred_element_type=F32)
        last = jnp.dot(outer[:, 2 * NNZ:], top[here], preferred_element_type=F32)
        width = last.shape[1]
        diag_out[0, k, 0] = (both[:, :width] + last).astype(BF16)
        lower_out[0, k, 0] = both[:, width:].astype(BF16)


def sandwich(own, below, above, even, weights, local, half, previous):
    left_w, own_w, right_w, outer = weights
    step, width = own.shape[1], outer.shape[0]
    count = min(4, step)
    base = half * step // count
    moving = pl.BlockSpec((1, count, NNZ, TILE), lambda p, g: (p, g, 0, 0))
    fixed = [pl.BlockSpec(w.shape, lambda p, g, n=w.ndim: (0,) * n) for w in (even,) + weights]
    out = jax.ShapeDtypeStruct((2, local, 1, width, width), BF16)
    out_spec = pl.BlockSpec((1, count, 1, width, width), lambda p, g: (p, base + g, 0, 0, 0))
    return pl.pallas_call(
        functools.partial(sandwich_body, count),
        grid=(2, step // count),
        out_shape=[out, out],
        in_specs=[moving] * 3 + fixed + [pl.BlockSpec(memory_space=pl.ANY)] * len(previous),
        out_specs=[out_spec, out_spec],
        input_output_aliases={8 + h: h for h in range(len(previous))},
        compiler_params=pltpu.CompilerParams(vmem_limit_bytes=48 << 20),
        cost_estimate=pl.CostEstimate(
            flops=2 * step * 2 * 1280 * 256 * 256,
            bytes_accessed=2 * step * (2 * width * width + 3 * NNZ * TILE) * 2,
            transcendentals=0,
        ),
        name="sandwich",
    )(own, below, above, even, left_w, own_w, right_w, outer, *previous)


def per_device(lesser, greater, vdiag, vlower, occupancy, tile_order):
    ranks = lax.axis_size("energy")
    local = lesser.shape[1]
    width = vdiag.shape[1]
    per_rank = NNZ // ranks
    late = max(1, per_rank // 4)
    chunks = [(0, per_rank - late), (per_rank - late, late)]
    halves = 2 if local >= 32 else 1
    counts, order = occupancy[0], tile_order[0]
    lesser = lesser.reshape(2, local, -1)
    greater = greater.reshape(2, local, -1)
    table = fourier_table(ranks * local)

    received = []
    for first, slots in chunks:
        packed, listing = pack(counts, order, lesser, greater, ranks, per_rank, first, slots)
        received.append(lax.all_to_all(packed, "energy", split_axis=0, concat_axis=0, tiled=True))

    diag_here, lower_here = vdiag[0], vlower[0]
    below_diag, below_list = passed_along((diag_here, listing), "space", 1)
    above_lower, above_list = passed_along((lower_here, listing), "space", -1)
    lists = jnp.stack([below_list, listing, above_list])
    even = (lists % 2 == 0).astype(F32)[:, :, None]
    rows = jnp.arange(width, dtype=jnp.int32)
    scatter = (rows[None, :, None] == (lists // 2)[:, None, :]).astype(BF16)
    outer = jnp.concatenate(
        [
            jnp.dot(lower_here, scatter[0], preferred_element_type=F32).astype(BF16),
            jnp.dot(diag_here, scatter[1], preferred_element_type=F32).astype(BF16),
            jnp.dot(above_lower.T, scatter[2], preferred_element_type=F32).astype(BF16),
        ],
        axis=1,
    )
    weights = (
        jnp.concatenate([lower_here.T, below_diag], axis=1),
        jnp.concatenate([diag_here, lower_here.T], axis=1),
        above_lower,
        outer,
    )

    polar = []
    for (first, _), data in zip(chunks, received):
        polar = correlate(table, data, per_rank, first, halves, polar)
    outs = []
    for h in range(halves):
        back = lax.all_to_all(polar[h], "energy", split_axis=0, concat_axis=0, tiled=True)
        own = back.reshape(NNZ, 2, local // halves, TILE).transpose(1, 2, 0, 3)
        below = passed_along(own, "space", 1)
        above = passed_along(own, "space", -1)
        outs = sandwich(own, below, above, even, weights, local, h, outs)
    return tuple(outs)


def solution(mesh):
    return jax.shard_map(
        per_device,
        mesh=mesh,
        in_specs=(
            P(None, "energy", "space", None),
            P(None, "energy", "space", None),
            P("space", None, None),
            P("space", None, None),
            P("space", None),
            P("space", None),
        ),
        out_specs=(P(None, "energy", "space", None, None), P(None, "energy", "space", None, None)),
        check_vma=False,
    )
```

time: 1510 us -> 402 us (0.27)
  matrix products: 458 us -> 1.99 us
  waiting for transfers between devices: 622 us -> 194 us
  local copies, waits for them, and re-layouts: 351 us -> 30.6 us
  Pallas kernels: 0 us -> 78.6 us
  blocking collectives: 0 us -> 52.2 us
  other arithmetic: 31.8 us -> 1.09 us
    dot_general x29 -> x3, matrix products: 458 us -> 1.99 us  [the longest x1 0.97 us: per_device(): jnp.dot(above_lower.T, scatter[2], preferred_element_type=F32).astype(BF16)]
    all_to_all x3, waiting for transfers between devices: 507 us -> 160 us  [the longest x2 147 us: per_device(): lax.all_to_all(packed, 'energy', split_axis=0, concat_axis=0, tiled=True)]
    reshape x7 -> x0, local copies, waits for them, and re-layouts: 163 us -> none  [the longest x2 77.6 us: pack(): tiled = source.reshape(2, local_energies, n_tiles, TILE)]
    ppermute x4 -> x8, waiting for transfers between devices: 115 us -> 34.1 us  [passed_along(): lax.ppermute(value, axis, [(source, source + steps) for source in range(l...]
    pallas_call x0 -> x6, Pallas kernels: none -> 78.6 us  [the longest x2 40.4 us: sandwich(): pl.pallas_call(functools.partial(sandwich_body, count), grid=(2, step //...]
    slice x4 -> x0, local copies, waits for them, and re-layouts: 54.1 us -> none  [the longest x2 44.3 us: unpack_tiles(): return field[:, :, :n_tiles, :].reshape(2, local_energies, width, width)]
    all_to_all x0 -> x1, blocking collectives: none -> 52.2 us  [per_device(): lax.all_to_all(polar[h], 'energy', split_axis=0, concat_axis=0, tiled=True)]
    scatter x1 -> x0, local copies, waits for them, and re-layouts: 40.8 us -> none  [unpack_tiles(): field = field.at[:, :, index, :].set(tiles)]
  transfers between devices with their start and end apart: 7 -> 11, of which waited for: 4 -> 6; matrix products, arithmetic and copies ran while one was open for 10% -> 2% of each run, Pallas kernels for 0% -> 11%
where the time goes in v1:
time: 402 us; the launch traced here: 400 us
  waiting for transfers between devices  194 us (48%)
  Pallas kernels  78.6 us (20%)
  blocking collectives  52.2 us (13%)
  starting transfers between devices  41 us (10%)
  local copies, waits for them, and re-layouts  30.6 us (8%)
    all_to_all x2, waiting for transfers between devices, per_device(): lax.all_to_all(packed, 'energy', split_axis=0, concat_axis=0, tiled=True)  147 us
    all_to_all x1, blocking collectives, per_device(): lax.all_to_all(polar[h], 'energy', split_axis=0, concat_axis=0, tiled=True)  52.2 us
    pallas_call x2, Pallas kernels, sandwich(): pl.pallas_call(functools.partial(sandwich_body, count), grid=(2, step //...  40.4 us
    ppermute x8, waiting for transfers between devices, passed_along(): lax.ppermute(value, axis, [(source, source + steps) for source in range(l...  34.1 us
    pallas_call x2, Pallas kernels, correlate(): pl.pallas_call(functools.partial(correlate_body, tiles, halves, float(ene...  27.5 us
    ppermute x8, starting transfers between devices, passed_along(): lax.ppermute(value, axis, [(source, source + steps) for source in range(l...  25.4 us
    unnamed x31, local copies, waits for them, and re-layouts  24.4 us
    all_to_all x1, waiting for transfers between devices, per_device(): lax.all_to_all(polar[h], 'energy', split_axis=0, concat_axis=0, tiled=True)  13.1 us
  transfers between devices with their start and end apart: 11, of which 6 were waited for; matrix products, arithmetic and copies ran while one was open for 2% of the time, Pallas kernels for 11%

profile of v1, /device:TPU:1, one launch (start us, length us, event | category | flops | bytes accessed | tf_op | source)
XLA Modules:
  0.0 400.2 jit_solution(16564607703911921245)
XLA Ops:
  0.6 5.8 %copy-done = bf16[2,64,1,65536]{3,1,2,0:T(8,128)(2,1)S(1)} copy-done((bf16[2,64,1,65536]{3,1,2,0:T(8,128)(2,1)S(1)}, bf16[2,64,1,65536]{3,1,2,0:T(8,128)(2,1)}, u32[]{:S(2)}) %copy-start) | copy-done | bytes 16777240
  7.7 5.5 %pack.3 = (bf16[8,12,2,2,64,128]{5,4,3,2,1,0:T(8,128)(2,1)S(1)}, s32[128]{0:T(128)}) custom-call(s32[8]{0:T(128)S(1)} %bitcast.50, s32[512]{0:T(512)S(1)} %bitcast.48, bf16[2,64,65536]{2,1,0:T(8,128)(2,1)S(1)} %bitcast.41, bf16[2,64,65536]{2,1,0:T(8,128)(2,1)} %bitcast.43), custom_call_target="tpu_custom_call" | custom-call | bytes 12582912 | tf_op jit(solution)/shard_map/pack/pallas_call | solution.py:61
  15.9 6.5 %all-to-all-start.1 = ((bf16[8,12,2,2,64,128]{5,4,3,2,1,0:T(8,128)(2,1)}), bf16[8,12,2,2,64,128]{5,4,3,2,1,0:T(8,128)(2,1)}, u32[]{:S(2)}, u32[]{:S(2)}) async-start(bf16[8,12,2,2,64,128]{5,4,3,2,1,0:T(8,128)(2,1)} %copy-done.3), calls=%async_computation.1 | async-start | bytes 12582912 | tf_op jit(solution)/shard_map/all_to_all | solution.py:209
  22.5 5.8 %copy-done.1 = bf16[2,64,1,65536]{3,1,2,0:T(8,128)(2,1)S(1)} copy-done((bf16[2,64,1,65536]{3,1,2,0:T(8,128)(2,1)S(1)}, bf16[2,64,1,65536]{3,1,2,0:T(8,128)(2,1)}, u32[]{:S(2)}) %copy-start.1) | copy-done | bytes 16777240
  28.2 5.8 %copy-done.2 = bf16[2,64,1,65536]{3,1,2,0:T(8,128)(2,1)S(1)} copy-done((bf16[2,64,1,65536]{3,1,2,0:T(8,128)(2,1)S(1)}, bf16[2,64,1,65536]{3,1,2,0:T(8,128)(2,1)}, u32[]{:S(2)}) %copy-start.2) | copy-done | bytes 16777240
  34.0 5.3 %pack.2 = (bf16[8,4,2,2,64,128]{5,4,3,2,1,0:T(8,128)(2,1)}, s32[128]{0:T(128)S(1)}) custom-call(s32[8]{0:T(128)S(1)} %bitcast.51, s32[512]{0:T(512)S(1)} %bitcast.49, bf16[2,64,65536]{2,1,0:T(8,128)(2,1)S(1)} %bitcast.42, bf16[2,64,65536]{2,1,0:T(8,128)(2,1)S(1)} %bitcast.44), custom_call_target="tpu_custom_call" | custom-call | bytes 4194304 | tf_op jit(solution)/shard_map/pack/pallas_call | solution.py:61
  39.3 120.5 %all-to-all-done.1.data = bf16[8,12,2,2,64,128]{5,4,3,2,1,0:T(8,128)(2,1)} async-done(((bf16[8,12,2,2,64,128]{5,4,3,2,1,0:T(8,128)(2,1)}), bf16[8,12,2,2,64,128]{5,4,3,2,1,0:T(8,128)(2,1)}, u32[]{:S(2)}, u32[]{:S(2)}) %all-to-all-start.1) | async-done | bytes 6291488 | tf_op jit(solution)/shard_map/all_to_all | solution.py:209
  159.8 4.7 %all-to-all-start = ((bf16[8,4,2,2,64,128]{5,4,3,2,1,0:T(8,128)(2,1)}), bf16[8,4,2,2,64,128]{5,4,3,2,1,0:T(8,128)(2,1)}, u32[]{:S(2)}, u32[]{:S(2)}) async-start(bf16[8,4,2,2,64,128]{5,4,3,2,1,0:T(8,128)(2,1)} %get-tuple-element.11), calls=%async_computation | async-start | bytes 4194304 | tf_op jit(solution)/shard_map/all_to_all | solution.py:209
  164.5 19.7 %correlate.2 = (bf16[8,16,2,32,128]{4,3,2,1,0:T(8,128)(2,1)S(1)}, bf16[8,16,2,32,128]{4,3,2,1,0:T(8,128)(2,1)S(1)}) custom-call(bf16[1024,1024]{1,0:T(8,128)(2,1)} %constant.29.clone.table, bf16[8,12,2,2,64,128]{5,4,3,2,1,0:T(8,128)(2,1)} %all-to-all-done.1.data), custom_call_target="tpu_custom_call" | custom-call | flops 9663676416 | bytes 12582912 | tf_op jit(solution)/shard_map/correlate/pallas_call | solution.py:126
  185.5 26.0 %all-to-all-done.data = bf16[8,4,2,2,64,128]{5,4,3,2,1,0:T(8,128)(2,1)} async-done(((bf16[8,4,2,2,64,128]{5,4,3,2,1,0:T(8,128)(2,1)}), bf16[8,4,2,2,64,128]{5,4,3,2,1,0:T(8,128)(2,1)}, u32[]{:S(2)}, u32[]{:S(2)}) %all-to-all-start) | async-done | bytes 2097184 | tf_op jit(solution)/shard_map/all_to_all | solution.py:209
  213.1 7.8 %correlate.3 = (bf16[8,16,2,32,128]{4,3,2,1,0:T(8,128)(2,1)S(1)}, bf16[8,16,2,32,128]{4,3,2,1,0:T(8,128)(2,1)S(1)}) custom-call(bf16[1024,1024]{1,0:T(8,128)(2,1)} %constant.29.clone.table, bf16[8,4,2,2,64,128]{5,4,3,2,1,0:T(8,128)(2,1)} %all-to-all-done.data, ...), custom_call_target="tpu_custom_call", output_to_operand_aliasing={{0}: (2, {}), {1}: (3, {})} | custom-call | flops 3221225472 | bytes 12582912 | tf_op jit(solution)/shard_map/correlate/pallas_call | solution.py:126
  221.0 52.2 %all_to_all.20 = bf16[8,16,2,32,128]{4,3,2,1,0:T(8,128)(2,1)} all-to-all(bf16[8,16,2,32,128]{4,3,2,1,0:T(8,128)(2,1)S(1)} %get-tuple-element.17), channel_id=1, replica_groups=mesh['energy'=8,'space'=4] {'energy'}, dimensions={0} | all-to-all | bytes 4194304 | tf_op jit(solution)/shard_map/all_to_all | solution.py:238
  273.2 4.5 %all-to-all-start.2 = ((bf16[8,16,2,32,128]{4,3,2,1,0:T(8,128)(2,1)}), bf16[8,16,2,32,128]{4,3,2,1,0:T(8,128)(2,1)}, u32[]{:S(2)}, u32[]{:S(2)}) async-start(bf16[8,16,2,32,128]{4,3,2,1,0:T(8,128)(2,1)} %copy-done.6), calls=%async_computation.2 | async-start | bytes 4194304 | tf_op jit(solution)/shard_map/all_to_all | solution.py:238
  280.4 3.8 collective-permute-start.7
  284.3 3.0 collective-permute-start.6
  289.9 3.0 collective-permute-start.2
  295.5 14.2 %collective-permute-done.3 = s32[128]{0:T(128)S(1)} collective-permute-done((s32[128]{0:T(128)S(1)}, s32[128]{0:T(128)S(1)}, u32[]{:S(2)}, u32[]{:S(2)}) %collective-permute-start.3) | collective-permute-done | bytes 544 | tf_op jit(solution)/shard_map/ppermute | solution.py:20
  311.1 13.1 %all-to-all-done.2 = bf16[8,16,2,32,128]{4,3,2,1,0:T(8,128)(2,1)} async-done(((bf16[8,16,2,32,128]{4,3,2,1,0:T(8,128)(2,1)}), bf16[8,16,2,32,128]{4,3,2,1,0:T(8,128)(2,1)}, u32[]{:S(2)}, u32[]{:S(2)}) %all-to-all-start.2) | async-done | bytes 2097184 | tf_op jit(solution)/shard_map/all_to_all | solution.py:238
  324.1 2.9 copy.26
  327.1 4.7 %collective-permute-start.1 = (bf16[2,32,128,128]{3,2,1,0:T(8,128)(2,1)S(1)}, bf16[2,32,128,128]{3,2,1,0:T(8,128)(2,1)}, u32[]{:S(2)}, u32[]{:S(2)}) collective-permute-start(bf16[2,32,128,128]{3,2,1,0:T(8,128)(2,1)S(1)} %bitcast.45), channel_id=1, source_target_pairs={{1,0},{2,1},{3,2},{5,4},{6,5},{7,6},{9,8},{10,9},{11,10},{13,12},{... | collective-permute-start | bytes 6291464 | tf_op jit(solution)/shard_map/ppermute | solution.py:20
  331.8 3.0 collective-permute-start
  339.0 19.0 %collective-permute-done.5.right_w = bf16[256,256]{1,0:T(8,128)(2,1)S(1)} collective-permute-done((bf16[256,256]{1,0:T(8,128)(2,1)S(1)}, bf16[256,256]{1,0:T(8,128)(2,1)S(1)}, u32[]{:S(2)}, u32[]{:S(2)}) %collective-permute-start.5) | collective-permute-done | bytes 131104 | tf_op jit(solution)/shard_map/ppermute | solution.py:20
  359.9 20.4 %sandwich.2 = (bf16[2,64,1,256,256]{4,3,2,1,0:T(8,128)(2,1)}, bf16[2,64,1,256,256]{4,3,2,1,0:T(8,128)(2,1)}) custom-call(bf16[2,32,128,128]{3,2,1,0:T(8,128)(2,1)} %bitcast.24.own, bf16[2,32,128,128]{3,2,1,0:T(8,128)(2,1)} %collective-permute-done.6.below, bf16[2,32,128,128]{3,2,1,0:T(8,128)(2,1)} %collective-permute-done.7.above, ...), custom_call_target="tpu_custom_call" | custom-call | flops 10737418240 | bytes 23068672 | tf_op jit(solution)/shard_map/sandwich/pallas_call | solution.py:176
  380.3 20.0 %sandwich.3 = (bf16[2,64,1,256,256]{4,3,2,1,0:T(8,128)(2,1)}, bf16[2,64,1,256,256]{4,3,2,1,0:T(8,128)(2,1)}) custom-call(bf16[2,32,128,128]{3,2,1,0:T(8,128)(2,1)S(1)} %bitcast.47, bf16[2,32,128,128]{3,2,1,0:T(8,128)(2,1)} %collective-permute-done.below, ...), custom_call_target="tpu_custom_call", output_to_operand_aliasing={{0}: (8, {}), {1}: (9, {})} | custom-call | flops 10737418240 | bytes 23068672 | tf_op jit(solution)/shard_map/sandwich/pallas_call | solution.py:176
  (51 shorter events, 22.1 us)
Async XLA Ops:
  0.6 5.8 %copy-start = (bf16[2,64,1,65536]{3,1,2,0:T(8,128)(2,1)S(1)}, bf16[2,64,1,65536]{3,1,2,0:T(8,128)(2,1)}, u32[]{:S(2)}) copy-start(bf16[2,64,1,65536]{3,1,2,0:T(8,128)(2,1)} %param.7) | copy-start | bytes 50331652
  13.2 2.7 copy-start.3
  15.9 6.5 %copy-start.8 = (s32[1,512]{1,0:T(1,128)S(1)}, s32[1,512]{1,0:T(1,128)}, u32[]{:S(2)}) copy-start(s32[1,512]{1,0:T(1,128)} %param.12) | copy-start | bytes 6148
  15.9 6.5 %copy-start.10 = (s32[1,8]{1,0:T(1,128)S(1)}, s32[1,8]{1,0:T(1,128)}, u32[]{:S(2)}) copy-start(s32[1,8]{1,0:T(1,128)} %param.11) | copy-start | bytes 100
  15.9 143.9 %all-to-all-start.1 = ((bf16[8,12,2,2,64,128]{5,4,3,2,1,0:T(8,128)(2,1)}), bf16[8,12,2,2,64,128]{5,4,3,2,1,0:T(8,128)(2,1)}, u32[]{:S(2)}, u32[]{:S(2)}) async-start(bf16[8,12,2,2,64,128]{5,4,3,2,1,0:T(8,128)(2,1)} %copy-done.3), calls=%async_computation.1 | async-start | bytes 12582912 | tf_op jit(solution)/shard_map/all_to_all | solution.py:209
  22.5 5.8 %copy-start.1 = (bf16[2,64,1,65536]{3,1,2,0:T(8,128)(2,1)S(1)}, bf16[2,64,1,65536]{3,1,2,0:T(8,128)(2,1)}, u32[]{:S(2)}) copy-start(bf16[2,64,1,65536]{3,1,2,0:T(8,128)(2,1)} %param.7) | copy-start | bytes 50331652
  28.2 5.8 %copy-start.2 = (bf16[2,64,1,65536]{3,1,2,0:T(8,128)(2,1)S(1)}, bf16[2,64,1,65536]{3,1,2,0:T(8,128)(2,1)}, u32[]{:S(2)}) copy-start(bf16[2,64,1,65536]{3,1,2,0:T(8,128)(2,1)} %param.8) | copy-start | bytes 50331652
  159.8 51.7 %all-to-all-start = ((bf16[8,4,2,2,64,128]{5,4,3,2,1,0:T(8,128)(2,1)}), bf16[8,4,2,2,64,128]{5,4,3,2,1,0:T(8,128)(2,1)}, u32[]{:S(2)}, u32[]{:S(2)}) async-start(bf16[8,4,2,2,64,128]{5,4,3,2,1,0:T(8,128)(2,1)} %get-tuple-element.11), calls=%async_computation | async-start | bytes 4194304 | tf_op jit(solution)/shard_map/all_to_all | solution.py:209
  184.2 1.3 copy-start.4
  211.5 1.6 copy-start.5
  221.0 52.2 %copy-start.6 = (bf16[8,16,2,32,128]{4,3,2,1,0:T(8,128)(2,1)}, bf16[8,16,2,32,128]{4,3,2,1,0:T(8,128)(2,1)S(1)}, u32[]{:S(2)}) copy-start(bf16[8,16,2,32,128]{4,3,2,1,0:T(8,128)(2,1)S(1)} %get-tuple-element.15) | copy-start | bytes 6291460
  273.2 4.5 %copy-start.11 = (bf16[8,16,2,32,128]{4,3,2,1,0:T(8,128)(2,1)S(1)}, bf16[8,16,2,32,128]{4,3,2,1,0:T(8,128)(2,1)}, u32[]{:S(2)}) copy-start(bf16[8,16,2,32,128]{4,3,2,1,0:T(8,128)(2,1)} %all_to_all.20) | copy-start | bytes 6291460
  273.2 50.9 %all-to-all-start.2 = ((bf16[8,16,2,32,128]{4,3,2,1,0:T(8,128)(2,1)}), bf16[8,16,2,32,128]{4,3,2,1,0:T(8,128)(2,1)}, u32[]{:S(2)}, u32[]{:S(2)}) async-start(bf16[8,16,2,32,128]{4,3,2,1,0:T(8,128)(2,1)} %copy-done.6), calls=%async_computation.2 | async-start | bytes 4194304 | tf_op jit(solution)/shard_map/all_to_all | solution.py:238
  277.7 15.3 %copy-start.13 = (bf16[1,256,256]{2,1,0:T(8,128)(2,1)S(1)}, bf16[1,256,256]{2,1,0:T(8,128)(2,1)}, u32[]{:S(2)}) copy-start(bf16[1,256,256]{2,1,0:T(8,128)(2,1)} %param.9) | copy-start | bytes 393220
  280.4 79.4 %collective-permute-start.7 = (bf16[2,32,128,128]{3,2,1,0:T(8,128)(2,1)}, bf16[2,32,128,128]{3,2,1,0:T(8,128)(2,1)}, u32[]{:S(2)}, u32[]{:S(2)}) collective-permute-start(bf16[2,32,128,128]{3,2,1,0:T(8,128)(2,1)} %bitcast.24.own), channel_id=1, source_target_pairs={{1,0},{2,1},{3,2},{5,4},{6,5},{7,6},{9,8},{10,9},{11,10},{13,12},{... | collective-permute-start | bytes 6291464 | tf_op jit(solution)/shard_map/ppermute | solution.py:20
  284.3 75.6 %collective-permute-start.6 = (bf16[2,32,128,128]{3,2,1,0:T(8,128)(2,1)}, bf16[2,32,128,128]{3,2,1,0:T(8,128)(2,1)}, u32[]{:S(2)}, u32[]{:S(2)}) collective-permute-start(bf16[2,32,128,128]{3,2,1,0:T(8,128)(2,1)} %bitcast.24.own), channel_id=1, source_target_pairs={{0,1},{1,2},{2,3},{4,5},{5,6},{6,7},{8,9},{9,10},{10,11},{12,13},{... | collective-permute-start | bytes 6291464 | tf_op jit(solution)/shard_map/ppermute | solution.py:20
  287.3 22.4 %collective-permute-start.3 = (s32[128]{0:T(128)S(1)}, s32[128]{0:T(128)S(1)}, u32[]{:S(2)}, u32[]{:S(2)}) collective-permute-start(s32[128]{0:T(128)S(1)} %get-tuple-element.16), channel_id=1, source_target_pairs={{1,0},{2,1},{3,2},{5,4},{6,5},{7,6},{9,8},{10,9},{11,10},{13,12},{... | collective-permute-start | bytes 1544 | tf_op jit(solution)/shard_map/ppermute | solution.py:20
  289.9 20.6 %collective-permute-start.2 = (s32[128]{0:T(128)S(1)}, s32[128]{0:T(128)S(1)}, u32[]{:S(2)}, u32[]{:S(2)}) collective-permute-start(s32[128]{0:T(128)S(1)} %get-tuple-element.16), channel_id=1, source_target_pairs={{0,1},{1,2},{2,3},{4,5},{5,6},{6,7},{8,9},{9,10},{10,11},{12,13},{... | collective-permute-start | bytes 1544 | tf_op jit(solution)/shard_map/ppermute | solution.py:20
  293.1 42.0 %collective-permute-start.4 = (bf16[256,256]{0,1:T(8,128)(2,1)S(1)}, bf16[256,256]{0,1:T(8,128)(2,1)S(1)}, u32[]{:S(2)}, u32[]{:S(2)}) collective-permute-start(bf16[256,256]{0,1:T(8,128)(2,1)S(1)} %bitcast.56), channel_id=1, source_target_pairs={{0,1},{1,2},{2,3},{4,5},{5,6},{6,7},{8,9},{9,10},{10,11},{12,13},{... | collective-permute-start | bytes 393224 | tf_op jit(solution)/shard_map/ppermute | solution.py:20
  311.0 24.1 %copy-start.12 = (bf16[1,256,256]{2,1,0:T(8,128)(2,1)S(1)}, bf16[1,256,256]{2,1,0:T(8,128)(2,1)}, u32[]{:S(2)}) copy-start(bf16[1,256,256]{2,1,0:T(8,128)(2,1)} %param.10) | copy-start | bytes 393220
  327.1 53.2 %collective-permute-start.1 = (bf16[2,32,128,128]{3,2,1,0:T(8,128)(2,1)S(1)}, bf16[2,32,128,128]{3,2,1,0:T(8,128)(2,1)}, u32[]{:S(2)}, u32[]{:S(2)}) collective-permute-start(bf16[2,32,128,128]{3,2,1,0:T(8,128)(2,1)S(1)} %bitcast.45), channel_id=1, source_target_pairs={{1,0},{2,1},{3,2},{5,4},{6,5},{7,6},{9,8},{10,9},{11,10},{13,12},{... | collective-permute-start | bytes 6291464 | tf_op jit(solution)/shard_map/ppermute | solution.py:20
  331.8 48.5 %collective-permute-start = (bf16[2,32,128,128]{3,2,1,0:T(8,128)(2,1)S(1)}, bf16[2,32,128,128]{3,2,1,0:T(8,128)(2,1)}, u32[]{:S(2)}, u32[]{:S(2)}) collective-permute-start(bf16[2,32,128,128]{3,2,1,0:T(8,128)(2,1)S(1)} %bitcast.46), channel_id=1, source_target_pairs={{0,1},{1,2},{2,3},{4,5},{5,6},{6,7},{8,9},{9,10},{10,11},{12,13},{... | collective-permute-start | bytes 6291464 | tf_op jit(solution)/shard_map/ppermute | solution.py:20
  334.9 3.8 copy-start.14
  335.1 22.9 %collective-permute-start.5 = (bf16[256,256]{1,0:T(8,128)(2,1)S(1)}, bf16[256,256]{1,0:T(8,128)(2,1)S(1)}, u32[]{:S(2)}, u32[]{:S(2)}) collective-permute-start(bf16[256,256]{1,0:T(8,128)(2,1)S(1)} %bitcast.54), channel_id=1, source_target_pairs={{1,0},{2,1},{3,2},{5,4},{6,5},{7,6},{9,8},{10,9},{11,10},{13,12},{... | collective-permute-start | bytes 393224 | tf_op jit(solution)/shard_map/ppermute | solution.py:20
  (2 other events, 1.3 us)

commit v2 on v1

--- a/solution.py
+++ b/solution.py
@@ -71,7 +71,7 @@
             pltpu.SemaphoreType.DMA,
             pltpu.SemaphoreType.DMA,
         ],
-        compiler_params=pltpu.CompilerParams(vmem_limit_bytes=16 << 20),
+        compiler_params=pltpu.CompilerParams(vmem_limit_bytes=60 << 20),
         cost_estimate=pl.CostEstimate(flops=0, bytes_accessed=moved, transcendentals=0),
         name="pack",
     )(counts, order, lesser, greater)
@@ -195,7 +195,7 @@
     local = lesser.shape[1]
     width = vdiag.shape[1]
     per_rank = NNZ // ranks
-    late = max(1, per_rank // 4)
+    late = max(1, per_rank // 8)
     chunks = [(0, per_rank - late), (per_rank - late, late)]
     halves = 2 if local >= 32 else 1
     counts, order = occupancy[0], tile_order[0]
@@ -203,10 +203,14 @@
     greater = greater.reshape(2, local, -1)
     table = fourier_table(ranks * local)
 
-    received = []
+    def exchanged(value):
+        return lax.all_to_all(value, "energy", split_axis=0, concat_axis=0, tiled=True)
+
+    packs = []
     for first, slots in chunks:
         packed, listing = pack(counts, order, lesser, greater, ranks, per_rank, first, slots)
-        received.append(lax.all_to_all(packed, "energy", split_axis=0, concat_axis=0, tiled=True))
+        packs.append(packed)
+    early = exchanged(packs[0])
 
     diag_here, lower_here = vdiag[0], vlower[0]
     below_diag, below_list = passed_along((diag_here, listing), "space", 1)
@@ -230,12 +234,15 @@
         outer,
     )
 
+    held = lax.optimization_barrier((packs[1], early, weights, even))
+    received = [held[1], exchanged(held[0])]
+    weights, even = held[2], held[3]
     polar = []
     for (first, _), data in zip(chunks, received):
         polar = correlate(table, data, per_rank, first, halves, polar)
     outs = []
     for h in range(halves):
-        back = lax.all_to_all(polar[h], "energy", split_axis=0, concat_axis=0, tiled=True)
+        back = exchanged(polar[h])
         own = back.reshape(NNZ, 2, local // halves, TILE).transpose(1, 2, 0, 3)
         below = passed_along(own, "space", 1)
         above = passed_along(own, "space", -1)

time: 402 us -> 369 us (0.918)
  local copies, waits for them, and re-layouts: 30.6 us -> 9.29 us
  waiting for transfers between devices: 194 us -> 181 us
    ppermute x8, waiting for transfers between devices: 34.1 us -> 4.79 us  [passed_along(): lax.ppermute(value, axis, [(source, source + steps) for source in range(l...]
    unnamed x31 -> x21, local copies, waits for them, and re-layouts: 24.4 us -> 3.04 us
    all_to_all x3, waiting for transfers between devices: 160 us -> 176 us  [exchanged(): lax.all_to_all(value, 'energy', split_axis=0, concat_axis=0, tiled=True)]
  transfers between devices with their start and end apart: 11 -> 11, of which waited for: 6 -> 6; matrix products, arithmetic and copies ran while one was open for 2% -> 3% of each run, Pallas kernels for 11% -> 13%
where the time goes in v2:
time: 369 us; the launch traced here: 367 us
  waiting for transfers between devices  181 us (49%)
  Pallas kernels  80.7 us (22%)
  blocking collectives  51.8 us (14%)
  starting transfers between devices  40.2 us (11%)
  local copies, waits for them, and re-layouts  9.29 us (3%)
    all_to_all x3, waiting for transfers between devices, exchanged(): lax.all_to_all(value, 'energy', split_axis=0, concat_axis=0, tiled=True)  176 us
    all_to_all x1, blocking collectives, exchanged(): lax.all_to_all(value, 'energy', split_axis=0, concat_axis=0, tiled=True)  51.8 us
    pallas_call x2, Pallas kernels, sandwich(): pl.pallas_call(functools.partial(sandwich_body, count), grid=(2, step //...  40.3 us
    pallas_call x2, Pallas kernels, correlate(): pl.pallas_call(functools.partial(correlate_body, tiles, halves, float(ene...  27.2 us
    ppermute x8, starting transfers between devices, passed_along(): lax.ppermute(value, axis, [(source, source + steps) for source in range(l...  24.7 us
    all_to_all x3, starting transfers between devices, exchanged(): lax.all_to_all(value, 'energy', split_axis=0, concat_axis=0, tiled=True)  15.6 us
    pallas_call x2, Pallas kernels, pack(): pl.pallas_call(functools.partial(pack_body, ranks, 2 * NNZ // ranks, per_...  13.2 us
  transfers between devices with their start and end apart: 11, of which 6 were waited for; matrix products, arithmetic and copies ran while one was open for 3% of the time, Pallas kernels for 13%

profile of v2, /device:TPU:1, one launch (start us, length us, event | category | flops | bytes accessed | tf_op | source)
XLA Modules:
  0.0 366.8 jit_solution(5282866671384006924)
XLA Ops:
  0.6 7.7 %pack.3 = (bf16[8,14,2,2,64,128]{5,4,3,2,1,0:T(8,128)(2,1)}, s32[128]{0:T(128)}) custom-call(s32[8]{0:T(128)} %bitcast.54, s32[512]{0:T(512)} %bitcast.52, bf16[2,64,65536]{2,1,0:T(8,128)(2,1)} %bitcast.44, bf16[2,64,65536]{2,1,0:T(8,128)(2,1)} %bitcast.46), custom_call_target="tpu_custom_call" | custom-call | bytes 14680064 | tf_op jit(solution)/shard_map/pack/pallas_call | solution.py:61
  8.3 6.4 %all-to-all-start = ((bf16[8,14,2,2,64,128]{5,4,3,2,1,0:T(8,128)(2,1)}), bf16[8,14,2,2,64,128]{5,4,3,2,1,0:T(8,128)(2,1)}, u32[]{:S(2)}, u32[]{:S(2)}) async-start(bf16[8,14,2,2,64,128]{5,4,3,2,1,0:T(8,128)(2,1)} %get-tuple-element.19), calls=%async_computation | async-start | bytes 14680064 | tf_op jit(solution)/shard_map/all_to_all | solution.py:207
  14.7 5.6 %pack.2 = (bf16[8,2,2,2,64,128]{5,4,3,2,1,0:T(8,128)(2,1)}, s32[128]{0:T(128)}) custom-call(s32[8]{0:T(128)} %bitcast.55, s32[512]{0:T(512)} %bitcast.53, bf16[2,64,65536]{2,1,0:T(8,128)(2,1)} %bitcast.45, bf16[2,64,65536]{2,1,0:T(8,128)(2,1)} %bitcast.47), custom_call_target="tpu_custom_call" | custom-call | bytes 2097152 | tf_op jit(solution)/shard_map/pack/pallas_call | solution.py:61
  20.3 2.9 collective-permute-start.3
  23.2 3.0 collective-permute-start.2
  26.3 2.4 collective-permute-start
  28.7 1.9 collective-permute-start.1
  32.9 2.5 collective-permute-done.1.right_w
  36.5 138.0 %all-to-all-done.data = bf16[8,14,2,2,64,128]{5,4,3,2,1,0:T(8,128)(2,1)} async-done(((bf16[8,14,2,2,64,128]{5,4,3,2,1,0:T(8,128)(2,1)}), bf16[8,14,2,2,64,128]{5,4,3,2,1,0:T(8,128)(2,1)}, u32[]{:S(2)}, u32[]{:S(2)}) %all-to-all-start) | async-done | bytes 7340064 | tf_op jit(solution)/shard_map/all_to_all | solution.py:207
  174.5 4.7 %all-to-all-start.1 = ((bf16[8,2,2,2,64,128]{5,4,3,2,1,0:T(8,128)(2,1)}), bf16[8,2,2,2,64,128]{5,4,3,2,1,0:T(8,128)(2,1)S(1)}, u32[]{:S(2)}, u32[]{:S(2)}) async-start(bf16[8,2,2,2,64,128]{5,4,3,2,1,0:T(8,128)(2,1)} %get-tuple-element.21), calls=%async_computation.1 | async-start | bytes 2097152 | tf_op jit(solution)/shard_map/all_to_all | solution.py:207
  179.2 22.6 %correlate.2 = (bf16[8,16,2,32,128]{4,3,2,1,0:T(8,128)(2,1)S(1)}, bf16[8,16,2,32,128]{4,3,2,1,0:T(8,128)(2,1)S(1)}) custom-call(bf16[1024,1024]{1,0:T(8,128)(2,1)} %constant.29.clone.table, bf16[8,14,2,2,64,128]{5,4,3,2,1,0:T(8,128)(2,1)} %all-to-all-done.data), custom_call_target="tpu_custom_call" | custom-call | flops 11274289152 | bytes 12582912 | tf_op jit(solution)/shard_map/correlate/pallas_call | solution.py:126
  204.3 1.6 copy-done.1
  205.9 4.6 %correlate.3 = (bf16[8,16,2,32,128]{4,3,2,1,0:T(8,128)(2,1)S(1)}, bf16[8,16,2,32,128]{4,3,2,1,0:T(8,128)(2,1)S(1)}) custom-call(bf16[1024,1024]{1,0:T(8,128)(2,1)} %constant.29.clone.table, bf16[8,2,2,2,64,128]{5,4,3,2,1,0:T(8,128)(2,1)S(1)} %all-to-all-done.1.data, ...), custom_call_target="tpu_custom_call", output_to_operand_aliasing={{0}: (2, {}), {1}: (3, {})} | custom-call | flops 1610612736 | bytes 12582912 | tf_op jit(solution)/shard_map/correlate/pallas_call | solution.py:126
  210.5 51.8 %all_to_all.20 = bf16[8,16,2,32,128]{4,3,2,1,0:T(8,128)(2,1)} all-to-all(bf16[8,16,2,32,128]{4,3,2,1,0:T(8,128)(2,1)S(1)} %get-tuple-element.31), channel_id=1, replica_groups=mesh['energy'=8,'space'=4] {'energy'}, dimensions={0} | all-to-all | bytes 4194304 | tf_op jit(solution)/shard_map/all_to_all | solution.py:207
  262.4 4.5 %all-to-all-start.2 = ((bf16[8,16,2,32,128]{4,3,2,1,0:T(8,128)(2,1)}), bf16[8,16,2,32,128]{4,3,2,1,0:T(8,128)(2,1)}, u32[]{:S(2)}, u32[]{:S(2)}) async-start(bf16[8,16,2,32,128]{4,3,2,1,0:T(8,128)(2,1)} %copy-done.2), calls=%async_computation.2 | async-start | bytes 4194304 | tf_op jit(solution)/shard_map/all_to_all | solution.py:207
  266.9 2.7 copy.36
  269.6 3.8 %collective-permute-start.7 = (bf16[2,32,128,128]{3,2,1,0:T(8,128)(2,1)}, bf16[2,32,128,128]{3,2,1,0:T(8,128)(2,1)}, u32[]{:S(2)}, u32[]{:S(2)}) collective-permute-start(bf16[2,32,128,128]{3,2,1,0:T(8,128)(2,1)} %bitcast.24.own), channel_id=1, source_target_pairs={{1,0},{2,1},{3,2},{5,4},{6,5},{7,6},{9,8},{10,9},{11,10},{13,12},{... | collective-permute-start | bytes 6291464 | tf_op jit(solution)/shard_map/ppermute | solution.py:20
  273.5 3.0 collective-permute-start.6
  276.5 36.9 %all-to-all-done.2 = bf16[8,16,2,32,128]{4,3,2,1,0:T(8,128)(2,1)} async-done(((bf16[8,16,2,32,128]{4,3,2,1,0:T(8,128)(2,1)}), bf16[8,16,2,32,128]{4,3,2,1,0:T(8,128)(2,1)}, u32[]{:S(2)}, u32[]{:S(2)}) %all-to-all-start.2) | async-done | bytes 2097184 | tf_op jit(solution)/shard_map/all_to_all | solution.py:207
  313.4 2.9 copy.35
  316.3 4.6 %collective-permute-start.5 = (bf16[2,32,128,128]{3,2,1,0:T(8,128)(2,1)S(1)}, bf16[2,32,128,128]{3,2,1,0:T(8,128)(2,1)}, u32[]{:S(2)}, u32[]{:S(2)}) collective-permute-start(bf16[2,32,128,128]{3,2,1,0:T(8,128)(2,1)S(1)} %bitcast.41), channel_id=1, source_target_pairs={{1,0},{2,1},{3,2},{5,4},{6,5},{7,6},{9,8},{10,9},{11,10},{13,12},{... | collective-permute-start | bytes 6291464 | tf_op jit(solution)/shard_map/ppermute | solution.py:20
  320.9 3.0 collective-permute-start.4
  324.3 20.4 %sandwich.2 = (bf16[2,64,1,256,256]{4,3,2,1,0:T(8,128)(2,1)}, bf16[2,64,1,256,256]{4,3,2,1,0:T(8,128)(2,1)}) custom-call(bf16[2,32,128,128]{3,2,1,0:T(8,128)(2,1)} %bitcast.24.own, bf16[2,32,128,128]{3,2,1,0:T(8,128)(2,1)} %collective-permute-done.6.below, bf16[2,32,128,128]{3,2,1,0:T(8,128)(2,1)} %collective-permute-done.7.above, ...), custom_call_target="tpu_custom_call" | custom-call | flops 10737418240 | bytes 23068672 | tf_op jit(solution)/shard_map/sandwich/pallas_call | solution.py:176
  346.9 19.9 %sandwich.3 = (bf16[2,64,1,256,256]{4,3,2,1,0:T(8,128)(2,1)}, bf16[2,64,1,256,256]{4,3,2,1,0:T(8,128)(2,1)}) custom-call(bf16[2,32,128,128]{3,2,1,0:T(8,128)(2,1)S(1)} %bitcast.43, bf16[2,32,128,128]{3,2,1,0:T(8,128)(2,1)} %collective-permute-done.4.below, ...), custom_call_target="tpu_custom_call", output_to_operand_aliasing={{0}: (8, {}), {1}: (9, {})} | custom-call | flops 10737418240 | bytes 23068672 | tf_op jit(solution)/shard_map/sandwich/pallas_call | solution.py:176
  (41 shorter events, 8.4 us)
Async XLA Ops:
  8.3 166.2 %all-to-all-start = ((bf16[8,14,2,2,64,128]{5,4,3,2,1,0:T(8,128)(2,1)}), bf16[8,14,2,2,64,128]{5,4,3,2,1,0:T(8,128)(2,1)}, u32[]{:S(2)}, u32[]{:S(2)}) async-start(bf16[8,14,2,2,64,128]{5,4,3,2,1,0:T(8,128)(2,1)} %get-tuple-element.19), calls=%async_computation | async-start | bytes 14680064 | tf_op jit(solution)/shard_map/all_to_all | solution.py:207
  14.7 11.5 %copy-start.9 = (bf16[1,256,256]{2,1,0:T(8,128)(2,1)S(1)}, bf16[1,256,256]{2,1,0:T(8,128)(2,1)}, u32[]{:S(2)}) copy-start(bf16[1,256,256]{2,1,0:T(8,128)(2,1)} %param.9) | copy-start | bytes 393220
  14.7 14.0 %copy-start.8 = (bf16[1,256,256]{2,1,0:T(8,128)(2,1)S(1)}, bf16[1,256,256]{2,1,0:T(8,128)(2,1)}, u32[]{:S(2)}) copy-start(bf16[1,256,256]{2,1,0:T(8,128)(2,1)} %param.10) | copy-start | bytes 393220
  20.3 10.4 %collective-permute-start.3 = (s32[128]{0:T(128)}, s32[128]{0:T(128)S(1)}, u32[]{:S(2)}, u32[]{:S(2)}) collective-permute-start(s32[128]{0:T(128)} %get-tuple-element.20), channel_id=1, source_target_pairs={{1,0},{2,1},{3,2},{5,4},{6,5},{7,6},{9,8},{10,9},{11,10},{13,12},{... | collective-permute-start | bytes 1544 | tf_op jit(solution)/shard_map/ppermute | solution.py:20
  23.2 7.5 %collective-permute-start.2 = (s32[128]{0:T(128)}, s32[128]{0:T(128)S(1)}, u32[]{:S(2)}, u32[]{:S(2)}) collective-permute-start(s32[128]{0:T(128)} %get-tuple-element.20), channel_id=1, source_target_pairs={{0,1},{1,2},{2,3},{4,5},{5,6},{6,7},{8,9},{9,10},{10,11},{12,13},{... | collective-permute-start | bytes 1544 | tf_op jit(solution)/shard_map/ppermute | solution.py:20
  26.3 9.4 %collective-permute-start = (bf16[256,256]{0,1:T(8,128)(2,1)S(1)}, bf16[256,256]{0,1:T(8,128)(2,1)S(1)}, u32[]{:S(2)}, u32[]{:S(2)}) collective-permute-start(bf16[256,256]{0,1:T(8,128)(2,1)S(1)} %bitcast.50), channel_id=1, source_target_pairs={{0,1},{1,2},{2,3},{4,5},{5,6},{6,7},{8,9},{9,10},{10,11},{12,13},{... | collective-permute-start | bytes 393224 | tf_op jit(solution)/shard_map/ppermute | solution.py:20
  28.7 6.7 %collective-permute-start.1 = (bf16[256,256]{1,0:T(8,128)(2,1)S(1)}, bf16[256,256]{1,0:T(8,128)(2,1)S(1)}, u32[]{:S(2)}, u32[]{:S(2)}) collective-permute-start(bf16[256,256]{1,0:T(8,128)(2,1)S(1)} %bitcast.48), channel_id=1, source_target_pairs={{1,0},{2,1},{3,2},{5,4},{6,5},{7,6},{9,8},{10,9},{11,10},{13,12},{... | collective-permute-start | bytes 393224 | tf_op jit(solution)/shard_map/ppermute | solution.py:20
  35.4 139.1 %copy-start.3 = (bf16[256,256]{1,0:T(8,128)(2,1)}, bf16[256,256]{1,0:T(8,128)(2,1)S(1)}, u32[]{:S(2)}) copy-start(bf16[256,256]{1,0:T(8,128)(2,1)S(1)} %collective-permute-done.1.right_w) | copy-start | bytes 393220
  174.5 29.8 %all-to-all-start.1 = ((bf16[8,2,2,2,64,128]{5,4,3,2,1,0:T(8,128)(2,1)}), bf16[8,2,2,2,64,128]{5,4,3,2,1,0:T(8,128)(2,1)S(1)}, u32[]{:S(2)}, u32[]{:S(2)}) async-start(bf16[8,2,2,2,64,128]{5,4,3,2,1,0:T(8,128)(2,1)} %get-tuple-element.21), calls=%async_computation.1 | async-start | bytes 2097152 | tf_op jit(solution)/shard_map/all_to_all | solution.py:207
  201.9 1.3 copy-start
  204.3 1.6 copy-start.1
  210.5 51.9 %copy-start.2 = (bf16[8,16,2,32,128]{4,3,2,1,0:T(8,128)(2,1)}, bf16[8,16,2,32,128]{4,3,2,1,0:T(8,128)(2,1)S(1)}, u32[]{:S(2)}) copy-start(bf16[8,16,2,32,128]{4,3,2,1,0:T(8,128)(2,1)S(1)} %get-tuple-element.25) | copy-start | bytes 6291460
  262.4 4.5 %copy-start.5 = (bf16[8,16,2,32,128]{4,3,2,1,0:T(8,128)(2,1)S(1)}, bf16[8,16,2,32,128]{4,3,2,1,0:T(8,128)(2,1)}, u32[]{:S(2)}) copy-start(bf16[8,16,2,32,128]{4,3,2,1,0:T(8,128)(2,1)} %all_to_all.20) | copy-start | bytes 6291460
  262.4 51.0 %all-to-all-start.2 = ((bf16[8,16,2,32,128]{4,3,2,1,0:T(8,128)(2,1)}), bf16[8,16,2,32,128]{4,3,2,1,0:T(8,128)(2,1)}, u32[]{:S(2)}, u32[]{:S(2)}) async-start(bf16[8,16,2,32,128]{4,3,2,1,0:T(8,128)(2,1)} %copy-done.2), calls=%async_computation.2 | async-start | bytes 4194304 | tf_op jit(solution)/shard_map/all_to_all | solution.py:207
  269.6 54.4 %copy-start.7 = (bf16[256,512]{0,1:T(8,128)(2,1)S(1)}, bf16[256,512]{0,1:T(8,128)(2,1)}, u32[]{:S(2)}) copy-start(bf16[256,512]{0,1:T(8,128)(2,1)} %get-tuple-element.27) | copy-start | bytes 786436
  269.6 54.5 %copy-start.6 = (bf16[256,512]{0,1:T(8,128)(2,1)S(1)}, bf16[256,512]{0,1:T(8,128)(2,1)}, u32[]{:S(2)}) copy-start(bf16[256,512]{0,1:T(8,128)(2,1)} %get-tuple-element.28) | copy-start | bytes 786436
  269.6 54.7 %copy-start.4 = (bf16[256,256]{1,0:T(8,128)(2,1)S(1)}, bf16[256,256]{1,0:T(8,128)(2,1)}, u32[]{:S(2)}) copy-start(bf16[256,256]{1,0:T(8,128)(2,1)} %copy-done.3) | copy-start | bytes 393220
  269.6 54.7 %collective-permute-start.7 = (bf16[2,32,128,128]{3,2,1,0:T(8,128)(2,1)}, bf16[2,32,128,128]{3,2,1,0:T(8,128)(2,1)}, u32[]{:S(2)}, u32[]{:S(2)}) collective-permute-start(bf16[2,32,128,128]{3,2,1,0:T(8,128)(2,1)} %bitcast.24.own), channel_id=1, source_target_pairs={{1,0},{2,1},{3,2},{5,4},{6,5},{7,6},{9,8},{10,9},{11,10},{13,12},{... | collective-permute-start | bytes 6291464 | tf_op jit(solution)/shard_map/ppermute | solution.py:20
  273.5 50.8 %collective-permute-start.6 = (bf16[2,32,128,128]{3,2,1,0:T(8,128)(2,1)}, bf16[2,32,128,128]{3,2,1,0:T(8,128)(2,1)}, u32[]{:S(2)}, u32[]{:S(2)}) collective-permute-start(bf16[2,32,128,128]{3,2,1,0:T(8,128)(2,1)} %bitcast.24.own), channel_id=1, source_target_pairs={{0,1},{1,2},{2,3},{4,5},{5,6},{6,7},{8,9},{9,10},{10,11},{12,13},{... | collective-permute-start | bytes 6291464 | tf_op jit(solution)/shard_map/ppermute | solution.py:20
  316.3 29.5 %collective-permute-start.5 = (bf16[2,32,128,128]{3,2,1,0:T(8,128)(2,1)S(1)}, bf16[2,32,128,128]{3,2,1,0:T(8,128)(2,1)}, u32[]{:S(2)}, u32[]{:S(2)}) collective-permute-start(bf16[2,32,128,128]{3,2,1,0:T(8,128)(2,1)S(1)} %bitcast.41), channel_id=1, source_target_pairs={{1,0},{2,1},{3,2},{5,4},{6,5},{7,6},{9,8},{10,9},{11,10},{13,12},{... | collective-permute-start | bytes 6291464 | tf_op jit(solution)/shard_map/ppermute | solution.py:20
  320.9 26.0 %collective-permute-start.4 = (bf16[2,32,128,128]{3,2,1,0:T(8,128)(2,1)S(1)}, bf16[2,32,128,128]{3,2,1,0:T(8,128)(2,1)}, u32[]{:S(2)}, u32[]{:S(2)}) collective-permute-start(bf16[2,32,128,128]{3,2,1,0:T(8,128)(2,1)S(1)} %bitcast.42), channel_id=1, source_target_pairs={{0,1},{1,2},{2,3},{4,5},{5,6},{6,7},{8,9},{9,10},{10,11},{12,13},{... | collective-permute-start | bytes 6291464 | tf_op jit(solution)/shard_map/ppermute | solution.py:20
